TPU v7x, 128 devices: a whole 4x4x4 slice. The times are simulated.
128 devices in a mesh: seq: 16 (over z, x), req: 8 (over y, core).
Axes of the slice: x: 4, y: 4, z: 4, core: 2. Of those that a mesh axis runs over, the one named last changes fastest.
Arguments:
- given_token_index: int32 [128], replicated, may hold values from 0 to 31999
- hidden: bfloat16 [128, 3584], P('req'), may hold values from -6 to 6
- token_embedding_table: bfloat16 [32000, 3584], P(('seq', 'req')), may hold values from -6 to 6
- attention_norm_gain: bfloat16 [7168], replicated, may hold values from 0.099609375 to 1.8984375
- query_key_value_weight: bfloat16 [7168, 10752], P('req', 'seq'), may hold values from -0.0625 to 0.0625
- rotated_key_cache: bfloat16 [96, 8, 128, 3584], P('seq', 'req'), may hold values from -240 to 240
- cached_value_pages: bfloat16 [96, 8, 128, 3584], P('seq', 'req'), may hold values from -6 to 6
- lengths: int32 [32], P('req'), may hold values from 1 to 6144, as said below
- request_page_slots: int32 [32, 48], P('req'), may hold values from 0 to 95, as said below
- attention_output_weight: bfloat16 [3584, 7168], P('seq'), may hold values from -0.375 to 0.375
- feedforward_norm_gain: bfloat16 [7168], replicated, may hold values from 0.099609375 to 1.8984375
- gate_weight: bfloat16 [7168, 14336], P('req', 'seq'), may hold values from -0.0625 to 0.0625
- up_weight: bfloat16 [7168, 14336], P('req', 'seq'), may hold values from -0.0625 to 0.0625
- adapter_down_map: bfloat16 [7168, 128], P('req'), may hold values from -0.0625 to 0.0625
- adapter_gate_map: bfloat16 [128, 14336], P(None, 'seq'), may hold values from -0.5 to 0.5
- adapter_up_map: bfloat16 [128, 14336], P(None, 'seq'), may hold values from -0.5 to 0.5
- down_weight: bfloat16 [14336, 7168], P('seq', 'req'), may hold values from -0.046875 to 0.046875
Outputs:
- block_out: bfloat16 [128, 7168], P('seq', 'req')
Inputs may be any that keep to these rules, and one draw needn't show every extreme that they name: `lengths`: in each group of 4 requests exactly one has 6144 tokens, and the pages of a group's requests number at most 96 together. `request_page_slots`: entry p of request i names a slot of its group, 0 to 95; the entries with p * 128 below lengths[i] are distinct within a group, the others name any slot. Slot g of a group lies on the seq index g // 6, at place g % 6.
All inputs are finite; a program needn't handle non-finite values.
Results may differ from a plain program's by a relative error of at most 0.028.
The roundings to bfloat16 on the way count: a program that leaves them out, or rounds other values in their place, can miss the bound.
Values may be sent and summed in bfloat16 or wider, within the bound.
A program may use at most 128 MiB of HBM per device.

v0:
```python
import math
import jax
import jax.numpy as jnp
from jax import lax
from jax.sharding import PartitionSpec as P

HEADS = 16
HD = 224
NEGATIVE = -1e30
EPSILON = 1e-05
ROTARY_BASE = 10000.0


def merged_2(array, axis, combine):
    everything = jax.tree.map(lambda part: lax.all_gather(part, axis), array)
    first = jax.tree.map(lambda part: part[0], everything)

    def hop(k, so_far):
        return combine(so_far, jax.tree.map(lambda part: part[k], everything))

    return lax.fori_loop(1, lax.axis_size(axis), hop, first)


def rms_norm(matrix, gain_vec):
    widened = matrix.astype(jnp.float32)
    factor = lax.rsqrt(jnp.mean(widened * widened, axis=-1, keepdims=True) + EPSILON)
    return (widened * factor * gain_vec.astype(jnp.float32)).astype(jnp.bfloat16)


def rotate(vectors, positions):
    half_dim = vectors.shape[-1] // 2
    frequency = ROTARY_BASE ** (-2.0 * jnp.arange(half_dim, dtype=jnp.float32) / vectors.shape[-1])
    angles = positions.astype(jnp.float32)[..., None, None] * frequency
    cosine = jnp.cos(angles)
    sine_part = jnp.sin(angles)
    front_half = vectors[..., :half_dim]
    back_half = vectors[..., half_dim:]
    return jnp.concatenate(
        [front_half * cosine - back_half * sine_part, back_half * cosine + front_half * sine_part],
        axis=-1,
    )


def softmax_join(earlier, later):
    first_max, first_sum, first_out = earlier
    second_max, second_sum, second_out = later
    overall = jnp.maximum(first_max, second_max)
    first_factor = jnp.exp(first_max - overall)
    second_factor = jnp.exp(second_max - overall)
    return (
        overall,
        first_sum * first_factor + second_sum * second_factor,
        first_out * first_factor[..., None] + second_out * second_factor[..., None],
    )


def body(
    given_token_index,
    hidden,
    token_embedding_table,
    attention_norm_gain,
    query_key_value_weight,
    rotated_key_cache,
    cached_value_pages,
    lengths,
    request_page_slots,
    attention_output_weight,
    feedforward_norm_gain,
    gate_weight,
    up_weight,
    adapter_down_map,
    adapter_gate_map,
    adapter_up_map,
    down_weight,
):
    seq_devices = lax.axis_size("seq")
    req_devices = lax.axis_size("req")
    seq_index = lax.axis_index("seq")
    req_index = lax.axis_index("req")
    group_rows = hidden.shape[0]
    requests = lengths.shape[0]
    steps_each = group_rows // requests
    vocab_rows = token_embedding_table.shape[0]
    first_id = (seq_index * req_devices + req_index) * vocab_rows
    local_ids = given_token_index - first_id
    present = (local_ids >= 0) & (local_ids < vocab_rows)
    looked = jnp.take(token_embedding_table, jnp.clip(local_ids, 0, vocab_rows - 1), axis=0).astype(
        jnp.float32
    )
    looked = jnp.where(present[:, None], looked, 0.0)
    everywhere = lax.psum(looked, ("seq", "req"))
    embedded = lax.dynamic_slice_in_dim(everywhere, req_index * group_rows, group_rows, 0)
    joined = jnp.concatenate([hidden, embedded.astype(jnp.bfloat16)], axis=1)
    normed = rms_norm(joined, attention_norm_gain)
    spread = lax.all_to_all(normed, "req", split_axis=1, concat_axis=0, tiled=True)
    block_rows = spread
    qkv_part = lax.psum_scatter(
        jnp.dot(block_rows, query_key_value_weight, preferred_element_type=jnp.float32),
        "req",
        scatter_dimension=0,
        tiled=True,
    )
    projected = lax.all_gather(qkv_part.astype(jnp.bfloat16), "seq", axis=1, tiled=True)
    head_cols = HEADS * HD
    queries = projected[:, :head_cols].reshape(requests, steps_each, HEADS, HD)
    new_keys = projected[:, head_cols : 2 * head_cols].reshape(requests, steps_each, HEADS, HD)
    new_values = projected[:, 2 * head_cols :].reshape(requests, steps_each, HEADS, HD)
    positions = lengths[:, None] + jnp.arange(steps_each, dtype=jnp.int32)[None, :]
    queries = rotate(queries.astype(jnp.float32), positions).astype(jnp.bfloat16)
    new_keys = rotate(new_keys.astype(jnp.float32), positions).astype(jnp.bfloat16)
    slots = rotated_key_cache.shape[0]
    page_len = rotated_key_cache.shape[2]
    cache_k = rotated_key_cache.reshape(slots * page_len, HEADS, HD)
    cache_v = cached_value_pages.reshape(slots * page_len, HEADS, HD)
    slot_ids = seq_index * slots + jnp.arange(slots, dtype=jnp.int32)
    page_ids = jnp.arange(request_page_slots.shape[1], dtype=jnp.int32)
    is_live = page_ids[None, :] < ((lengths + page_len - 1) // page_len)[:, None]
    matches = (request_page_slots[:, :, None] == slot_ids[None, None, :]) & is_live[:, :, None]
    is_owned = jnp.any(matches, axis=1)
    page_of = jnp.sum(jnp.where(matches, page_ids[None, :, None], 0), axis=1)
    token_pos = (
        page_of[:, :, None] * page_len + jnp.arange(page_len, dtype=jnp.int32)[None, None, :]
    )
    is_valid = (is_owned[:, :, None] & (token_pos < lengths[:, None, None])).reshape(
        requests, slots * page_len
    )
    score_scale = 1.0 / math.sqrt(HD)
    scores = (
        jnp.einsum("rthd,khd->rthk", queries, cache_k, preferred_element_type=jnp.float32)
        * score_scale
    )
    mask_b = is_valid[:, None, None, :]
    local_max = jnp.max(jnp.where(mask_b, scores, NEGATIVE), axis=-1)
    weights = jnp.where(mask_b, jnp.exp(scores - local_max[..., None]), 0.0)
    local_sum = jnp.sum(weights, axis=-1)
    local_out = jnp.einsum(
        "rthk,khd->rthd", weights.astype(jnp.bfloat16), cache_v, preferred_element_type=jnp.float32
    )
    fresh_scores = (
        jnp.einsum("rthd,rshd->rths", queries, new_keys, preferred_element_type=jnp.float32)
        * score_scale
    )
    causal = jnp.arange(steps_each)[:, None] >= jnp.arange(steps_each)[None, :]
    fresh_mask = causal[None, :, None, :]
    fresh_max = jnp.max(jnp.where(fresh_mask, fresh_scores, NEGATIVE), axis=-1)
    fresh_w = jnp.where(fresh_mask, jnp.exp(fresh_scores - fresh_max[..., None]), 0.0)
    fresh_sum = jnp.sum(fresh_w, axis=-1)
    fresh_out = jnp.einsum(
        "rths,rshd->rthd",
        fresh_w.astype(jnp.bfloat16),
        new_values,
        preferred_element_type=jnp.float32,
    )
    own_heads = HEADS // seq_devices
    first_head = seq_index * own_heads

    def own_slice(member):
        return lax.dynamic_slice_in_dim(member, first_head, own_heads, 2)

    fresh_part = (own_slice(fresh_max), own_slice(fresh_sum), own_slice(fresh_out))
    merged = merged_2((local_max, local_sum, local_out), "seq", softmax_join)
    combined = softmax_join(tuple((own_slice(member) for member in merged)), fresh_part)
    attention = (
        (combined[2] / combined[1][..., None])
        .astype(jnp.bfloat16)
        .reshape(group_rows, own_heads * HD)
    )
    projected_out = jnp.dot(attention, attention_output_weight, preferred_element_type=jnp.float32)
    mixed_sum = lax.psum(projected_out, "seq")
    after_attn = (joined.astype(jnp.float32) + mixed_sum).astype(jnp.bfloat16)
    second_normed_state = rms_norm(after_attn, feedforward_norm_gain)
    residual_cols, second_spread_state = (
        lax.all_to_all(after_attn, "req", split_axis=1, concat_axis=0, tiled=True),
        lax.all_to_all(second_normed_state, "req", split_axis=1, concat_axis=0, tiled=True),
    )
    gate_total, up_total, low_sum = lax.psum(
        (
            jnp.dot(second_spread_state, gate_weight, preferred_element_type=jnp.float32),
            jnp.dot(second_spread_state, up_weight, preferred_element_type=jnp.float32),
            jnp.dot(second_spread_state, adapter_down_map, preferred_element_type=jnp.float32),
        ),
        "req",
    )
    adapter_hidden = low_sum.astype(jnp.bfloat16)
    gate_preactivation = gate_total + jnp.dot(
        adapter_hidden, adapter_gate_map, preferred_element_type=jnp.float32
    )
    up_projection_part = up_total + jnp.dot(
        adapter_hidden, adapter_up_map, preferred_element_type=jnp.float32
    )
    inner_act = (jax.nn.silu(gate_preactivation) * up_projection_part).astype(jnp.bfloat16)
    out_rows = residual_cols.shape[0] // seq_devices
    block_rows = inner_act
    down_sum = lax.psum_scatter(
        jnp.dot(block_rows, down_weight, preferred_element_type=jnp.float32),
        "seq",
        scatter_dimension=0,
        tiled=True,
    )
    residual_rows = lax.dynamic_slice_in_dim(residual_cols, seq_index * out_rows, out_rows, 0)
    return (residual_rows.astype(jnp.float32) + down_sum).astype(jnp.bfloat16)


def solution(mesh):
    placed = (
        P(),
        P("req", None),
        P(("seq", "req"), None),
        P(),
        P("req", "seq"),
        P("seq", "req", None, None),
        P("seq", "req", None, None),
        P("req"),
        P("req", None),
        P("seq", None),
        P(),
        P("req", "seq"),
        P("req", "seq"),
        P("req", None),
        P(None, "seq"),
        P(None, "seq"),
        P("seq", "req"),
    )
    return jax.shard_map(
        body, mesh=mesh, in_specs=placed, out_specs=P("seq", "req"), check_vma=False
    )
```

profile of v0, /device:TPU:0, one launch (start us, length us, event | category | flops | bytes accessed | tf_op | source)
XLA Modules:
  0.0 529.0 jit_solution(585776612457046075)
XLA Ops:
  7.4 4.9 gather_fusion
  12.2 2.8 convert_select_fusion
  15.0 74.1 %all-reduce.12 = bf16[128,3584]{1,0:T(8,128)(2,1)} all-reduce(f32[128,3584]{1,0:T(8,128)} %convert_select_fusion), channel_id=1, replica_groups=mesh['seq'=16,'req'=8] {'seq','req'}, use_global_device_ids=true, to_apply=%region_0.1 | all-reduce | flops 458752 | bytes 2752512 | tf_op jit(solution)/shard_map/psum | solution.py:91
  92.9 1.0 multiply_convert_fusion
  94.6 3.9 all-to-all-start
  100.2 1.5 fusion.55
  102.9 1.3 copy.111
  104.2 1.3 broadcast_bitcast_fusion.1
  105.4 1.3 add_convert_fusion.2
  106.7 2.6 fusion.67
  110.2 13.1 %reshape.185 = bf16[768,16,224]{2,1,0:T(8,128)(2,1)} reshape(bf16[6,1,128,3584]{3,2,1,0:T(8,128)(2,1)} %param.24) | data formatting | bytes 11010048 | tf_op jit(solution)/shard_map/reshape | solution.py:113
  123.3 13.2 %reshape.186 = bf16[768,16,224]{2,1,0:T(8,128)(2,1)} reshape(bf16[6,1,128,3584]{3,2,1,0:T(8,128)(2,1)} %param.25) | data formatting | bytes 11010048 | tf_op jit(solution)/shard_map/reshape | solution.py:114
  138.0 1.1 reduce-scatter.2.cloned.1.call-done
  139.9 24.2 %all-gather.3 = bf16[16,672,16]{1,2,0:T(8,128)(2,1)S(1)} all-gather(bf16[1,672,16]{1,2,0:T(8,128)(2,1)S(1)} %convert_bitcast_fusion), channel_id=1, replica_groups=mesh['seq'=16,'req'=8] {'seq'}, dimensions={0}, use_global_device_ids=true | all-gather | bytes 365568 | tf_op jit(solution)/shard_map/all_gather | solution.py:103
  165.0 1.5 reshape.211
  167.4 1.1 reshape.191
  169.3 1.1 reshape.190
  170.6 1.3 subtract_convert_fusion
  171.9 6.8 %select_reduce_fusion = (f32[4,4,16]{1,0,2:T(4,128)S(1)}, f32[4,4,16,768]{3,1,0,2:T(4,128)S(1)}) fusion(pred[4,768]{1,0:T(4,128)(4,1)} %fusion.54, bf16[768,16,224,1]{2,1,0,3:T(8,128)(2,1)} %bitcast.116, bf16[4,4,16,112]{3,1,0,2:T(4,128)(2,1)S(1)} %get-tuple-element.268, bf16[4,4,16,112]{3,1,0,2:T(4,128)(2,1)S(1)} %get-tuple-element.269), kind=kOutput, calls=%fused_computation.25 | convolution fusion | flops 88899328 | bytes 6410240 | tf_op jit(solution)/shard_map/rthd,khd->rthk/dot_general | solution.py:129
  179.7 4.6 fusion.16
  185.6 2.3 fusion.21
  188.7 22.9 %all-gather.1 = f32[64,4,16]{2,1,0:T(4,128)S(1)} all-gather(f32[4,4,16]{2,1,0:T(4,128)S(1)} %copy.119), channel_id=3, replica_groups=mesh['seq'=16,'req'=8] {'seq'}, dimensions={0}, use_global_device_ids=true | all-gather | bytes 17408 | tf_op jit(solution)/shard_map/all_gather | solution.py:15
  211.7 21.9 %all-gather = f32[64,4,16]{2,1,0:T(4,128)S(1)} all-gather(f32[4,4,16]{2,1,0:T(4,128)} %copy.118), channel_id=2, replica_groups=mesh['seq'=16,'req'=8] {'seq'}, dimensions={0}, use_global_device_ids=true | all-gather | bytes 17408 | tf_op jit(solution)/shard_map/all_gather | solution.py:15
  233.6 1.2 pad_maximum_fusion.1
  235.7 1.1 copy.129
  242.3 29.8 %while.19 = (s32[]{:T(128)}, f32[4,4,16]{2,1,0:T(4,128)S(1)}, f32[4,4,16]{2,1,0:T(4,128)S(1)}, f32[4,4,16,224]{3,2,1,0:T(8,128)S(1)}, f32[16,4,4,16]{3,2,1,0:T(4...) while((s32[]{:T(128)}, f32[4,4,16]{2,1,0:T(4,128)S(1)}, ...), condition=%wide.region_8.9_spmd, body=%wide.region_7.8_spmd.sunk | while | flops 173573 | bytes 1157271 | solution.py:21
  243.0 1.0 constant_dynamic-slice_fusion.5
  245.0 1.0 constant_dynamic-slice_fusion.5
  247.0 1.0 constant_dynamic-slice_fusion.5
  249.0 1.0 constant_dynamic-slice_fusion.5
  251.0 1.0 constant_dynamic-slice_fusion.5
  253.0 1.0 constant_dynamic-slice_fusion.5
  270.9 1.0 constant_dynamic-slice_fusion.5
  274.1 1.3 fusion.68
  275.5 81.3 %all-reduce.7.cloned.1.call-done = f32[16,7168]{1,0:T(8,128)} async-done(((f32[16,7168]{1,0:T(8,128)}), f32[16,7168]{1,0:T(8,128)}) %all-reduce.7.cloned.1.call-update) | async-done | bytes 458768 | tf_op jit(solution)/shard_map/psum | solution.py:169
  356.7 1.3 fusion.24
  358.2 11.4 %all_to_all.54 = bf16[16,8,896]{2,0,1:T(8,128)(2,1)S(1)} all-to-all(bf16[16,8,896]{2,0,1:T(8,128)(2,1)S(1)} %bitcast.125), channel_id=1, replica_groups=mesh['seq'=16,'req'=8] {'req'}, dimensions={1} | all-to-all | bytes 458752 | tf_op jit(solution)/shard_map/all_to_all | solution.py:174
  369.7 1.2 fusion.69
  370.9 1.2 fusion.71
  372.2 1.2 fusion.70
  373.4 24.2 %psum.38 = bf16[128,128]{1,0:T(8,128)(2,1)S(1)} all-reduce(f32[128,128]{1,0:T(8,128)S(1)} %fusion.70), channel_id=1, replica_groups=mesh['seq'=16,'req'=8] {'req'}, use_global_device_ids=true, to_apply=%region_14.15 | all-reduce | flops 16384 | bytes 98304 | tf_op jit(solution)/shard_map/psum | solution.py:176
  397.5 34.2 %all-reduce.11.cloned.1.call-done = (f32[128,896]{1,0:T(8,128)}, f32[128,896]{1,0:T(8,128)}) async-done(((f32[128,896]{1,0:T(8,128)}, f32[128,896]{1,0:T(8,128)}), (f32[128,896]{1,0:T(8,128)}, f32[128,896]{1,0:T(8,128)})) %all-reduce.11.cloned.1.call-update) | async-done | bytes 917520 | tf_op jit(solution)/shard_map/psum | solution.py:176
  431.8 2.1 convolution_add_fusion.1
  433.9 3.2 fusion.19
  437.9 3.4 all-to-all-start.1
  442.5 5.9 %all-to-all-done.1 = bf16[16,8,896]{2,0,1:T(8,128)(2,1)S(1)} async-done(((bf16[16,8,896]{2,0,1:T(8,128)(2,1)}), bf16[16,8,896]{2,0,1:T(8,128)(2,1)S(1)}, u32[]{:S(2)}, u32[]{:S(2)}) %all-to-all-start.1) | async-done | bytes 229408 | tf_op jit(solution)/shard_map/all_to_all | solution.py:173
  448.4 72.7 %all-reduce.9.cloned.1.call-done = f32[128,896]{1,0:T(8,128)} async-done(((f32[128,896]{1,0:T(8,128)}), f32[128,896]{1,0:T(8,128)}) %all-reduce.9.cloned.1.call-update) | async-done | bytes 458768
  521.1 1.4 fusion.45
  (155 shorter events, 49.5 us)
Async XLA Ops:
  6.5 267.5 %copy-start = (bf16[224,7168]{1,0:T(8,128)(2,1)S(1)}, bf16[224,7168]{1,0:T(8,128)(2,1)}, u32[]{:S(2)}) copy-start(bf16[224,7168]{1,0:T(8,128)(2,1)} %param.28) | copy-start | bytes 9633796
  15.0 75.1 %copy-start.7 = (bf16[16,3584]{1,0:T(8,128)(2,1)S(1)}, bf16[16,3584]{1,0:T(8,128)(2,1)}, u32[]{:S(2)}) copy-start(bf16[16,3584]{1,0:T(8,128)(2,1)} %param.20) | copy-start | bytes 344068
  90.0 19.3 %copy-start.3 = (bf16[16,3584]{1,0:T(8,128)(2,1)}, bf16[16,3584]{1,0:T(8,128)(2,1)S(1)}, u32[]{:S(2)}) copy-start(bf16[16,3584]{1,0:T(8,128)(2,1)S(1)} %dynamic-slice_convert_fusion) | copy-start | bytes 344068
  94.6 12.1 %all-to-all-start = ((bf16[16,8,896]{2,0,1:T(8,128)(2,1)}), bf16[16,8,896]{2,0,1:T(8,128)(2,1)S(1)}, u32[]{:S(2)}, u32[]{:S(2)}) async-start(bf16[16,8,896]{2,0,1:T(8,128)(2,1)} %copy.113), calls=%async_computation | async-start | bytes 458752 | tf_op jit(solution)/shard_map/all_to_all | solution.py:95
  98.5 40.6 %reduce-scatter.2.cloned.1.call-start = ((), (), s32[]{:S(2)}) async-start(), calls=%async_computation.4 | async-start | bytes 442368 | tf_op jit(solution)/shard_map/reduce_scatter | solution.py:97
  109.3 131.8 %all-gather.6.cloned.1.call-start = ((), (), s32[]{:S(2)}) async-start(), calls=%async_computation.6 | async-start | bytes 4456448 | tf_op jit(solution)/shard_map/all_gather | solution.py:15
  123.3 13.2 %copy-start.20 = (f32[4,4]{1,0:T(4,128)S(1)}, f32[4,4]{1,0:T(4,128)}, u32[]{:S(2)}) copy-start(f32[4,4]{1,0:T(4,128)} %add_convert_fusion.2) | copy-start | bytes 196
  123.3 14.0 %copy-start.16 = (s32[768]{0:T(1024)S(1)}, s32[768]{0:T(1024)}, u32[]{:S(2)}) copy-start(s32[768]{0:T(1024)} %iota_bitcast_fusion) | copy-start | bytes 9220
  123.3 14.0 %copy-start.17 = (pred[1,4,6,128]{3,2,1,0:T(8,128)(4,1)S(1)}, pred[1,4,6,128]{3,2,1,0:T(8,128)(4,1)}, u32[]{:S(2)}) copy-start(pred[1,4,6,128]{3,2,1,0:T(8,128)(4,1)} %broadcast_bitcast_fusion.1) | copy-start | bytes 9220
  123.3 14.0 %copy-start.21 = (s32[4]{0:T(128)S(1)}, s32[4]{0:T(128)}, u32[]{:S(2)}) copy-start(s32[4]{0:T(128)} %param.26) | copy-start | bytes 52
  167.4 3.1 copy-start.14
  167.4 3.1 copy-start.15
  170.5 9.2 %slice-start = ((s8[6291456]{0:T(1024)(128)(4,1)}), s8[4194304]{0:T(1024)(128)(4,1)S(1)}, s32[]{:S(2)}) async-start(s8[6291456]{0:T(1024)(128)(4,1)} %bitcast.113), calls=%async_computation.9 | async-start | bytes 8388608
  171.9 6.9 %copy-start.11 = (bf16[4,4,16,112]{3,1,0,2:T(4,128)(2,1)}, bf16[4,4,16,112]{3,1,0,2:T(4,128)(2,1)S(1)}, u32[]{:S(2)}) copy-start(bf16[4,4,16,112]{3,1,0,2:T(4,128)(2,1)S(1)} %get-tuple-element.269) | copy-start | bytes 172036
  171.9 7.8 %slice-start.1 = ((s8[6291456]{0:T(1024)(128)(4,1)}), s8[2097152]{0:T(1024)(128)(4,1)S(1)}, s32[]{:S(2)}) async-start(s8[6291456]{0:T(1024)(128)(4,1)} %bitcast.113), calls=%async_computation.10 | async-start | bytes 4194304
  171.9 7.8 %copy-start.19 = (pred[4,768]{1,0:T(4,128)(4,1)S(1)}, pred[4,768]{1,0:T(4,128)(4,1)}, u32[]{:S(2)}) copy-start(pred[4,768]{1,0:T(4,128)(4,1)} %fusion.54) | copy-start | bytes 9220
  178.8 0.9 copy-start.9
  184.3 55.7 %copy-start.10 = (bf16[16,3584]{1,0:T(8,128)(2,1)S(1)}, bf16[16,3584]{1,0:T(8,128)(2,1)}, u32[]{:S(2)}) copy-start(bf16[16,3584]{1,0:T(8,128)(2,1)} %get-tuple-element.255) | copy-start | bytes 344068
  184.3 172.4 %all-reduce.7.cloned.1.call-start = ((), (), s32[]{:S(2)}) async-start(), calls=%async_computation.5 | async-start | bytes 917504 | tf_op jit(solution)/shard_map/psum | solution.py:169
  211.7 23.1 %copy-start.12 = (f32[64,4,16]{2,1,0:T(4,128)}, f32[64,4,16]{2,1,0:T(4,128)S(1)}, u32[]{:S(2)}) copy-start(f32[64,4,16]{2,1,0:T(4,128)S(1)} %all-gather.1) | copy-start | bytes 49156
  233.6 1.2 copy-start.13
  274.0 1.4 copy-start.18
  274.0 82.7 %copy-start.4 = (bf16[16,3584]{1,0:T(8,128)(2,1)S(1)}, bf16[16,3584]{1,0:T(8,128)(2,1)}, u32[]{:S(2)}) copy-start(bf16[16,3584]{1,0:T(8,128)(2,1)} %copy-done.3) | copy-start | bytes 344068
  274.1 82.7 %copy-start.8 = (bf16[16,3584]{1,0:T(8,128)(2,1)S(1)}, bf16[16,3584]{1,0:T(8,128)(2,1)}, u32[]{:S(2)}) copy-start(bf16[16,3584]{1,0:T(8,128)(2,1)} %param.20) | copy-start | bytes 344068
  275.4 156.4 %all-reduce.11.cloned.1.call-start = ((), (), s32[]{:S(2)}) async-start(), calls=%async_computation.8 | async-start | bytes 1835008 | tf_op jit(solution)/shard_map/psum | solution.py:176
  356.7 12.9 %copy-start.5 = (bf16[896,896]{1,0:T(8,128)(2,1)S(1)}, bf16[896,896]{1,0:T(8,128)(2,1)}, u32[]{:S(2)}) copy-start(bf16[896,896]{1,0:T(8,128)(2,1)} %param.30) | copy-start | bytes 4816900
  358.1 12.9 %copy-start.1 = (bf16[16,7168]{1,0:T(8,128)(2,1)}, bf16[16,7168]{1,0:T(8,128)(2,1)S(1)}, u32[]{:S(2)}) copy-start(bf16[16,7168]{1,0:T(8,128)(2,1)S(1)} %get-tuple-element.249) | copy-start | bytes 688132
  358.1 12.8 %copy-start.6 = (bf16[896,896]{1,0:T(8,128)(2,1)S(1)}, bf16[896,896]{1,0:T(8,128)(2,1)}, u32[]{:S(2)}) copy-start(bf16[896,896]{1,0:T(8,128)(2,1)} %param.31) | copy-start | bytes 4816900
  372.2 148.9 %all-reduce.9.cloned.1.call-start = ((), (), s32[]{:S(2)}) async-start(), calls=%async_computation.7 | async-start | bytes 917504
  433.9 3.2 copy-start.2
  433.9 7.3 %copy-start.22 = (u32[128]{0:T(128)S(1)}, u32[128]{0:T(128)}, u32[]{:S(2)}) copy-start(u32[128]{0:T(128)} %constant.127) | copy-start | bytes 1540
  437.9 10.5 %all-to-all-start.1 = ((bf16[16,8,896]{2,0,1:T(8,128)(2,1)}), bf16[16,8,896]{2,0,1:T(8,128)(2,1)S(1)}, u32[]{:S(2)}, u32[]{:S(2)}) async-start(bf16[16,8,896]{2,0,1:T(8,128)(2,1)} %bitcast.123), calls=%async_computation.2 | async-start | bytes 458752 | tf_op jit(solution)/shard_map/all_to_all | solution.py:173
Sparse Core Ops, SparseCore 0:
  109.4 29.5 reduce-scatter.1
  184.4 48.8 all-gather.5
  275.5 81.1 all-reduce.6
  372.3 59.4 all-reduce.10
  437.3 83.7 all-reduce.8
where the time goes:
time: 532 us; the launch traced here: 529 us
  waiting for transfers between devices  195 us (37%)
  blocking collectives  179 us (34%)
  local copies, waits for them, and re-layouts  66.7 us (13%)
  other arithmetic  40.1 us (8%)
  matrix products  26 us (5%)
  between operations  14.2 us (3%)
  starting transfers between devices  7.46 us (1%)
    psum x1, waiting for transfers between devices, body(): mixed_sum = lax.psum(projected_out, 'seq')  81.3 us
    psum x1, blocking collectives, body(): everywhere = lax.psum(looked, ('seq', 'req'))  74.1 us
    unnamed x6, waiting for transfers between devices  72.8 us
    all_gather x2, blocking collectives, merged_2(): everything = jax.tree.map(lambda part: lax.all_gather(part, axis), array)  44.8 us
    psum x1, waiting for transfers between devices, body(): lax.psum((jnp.dot(second_spread_state, gate_weight, preferred_element_typ...  34.2 us
    all_gather x1, blocking collectives, body(): lax.all_gather(qkv_part.astype(jnp.bfloat16), 'seq', axis=1, tiled=True)  24.2 us
    psum x1, blocking collectives, body(): lax.psum((jnp.dot(second_spread_state, gate_weight, preferred_element_typ...  24.2 us
    dynamic_slice x15, local copies, waits for them, and re-layouts, hop(): return combine(so_far, jax.tree.map(lambda part: part[k], everything))  14.7 us
  transfers between devices with their start and end apart: 7, of which 5 were waited for; matrix products, arithmetic and copies ran while one was open for 10% of the time, Pallas kernels for 0%

commit v1 on v0

--- a/solution.py
+++ b/solution.py
@@ -100,7 +100,12 @@
         scatter_dimension=0,
         tiled=True,
     )
-    projected = lax.all_gather(qkv_part.astype(jnp.bfloat16), "seq", axis=1, tiled=True)
+    projected = jnp.concatenate(
+        lax.all_to_all(
+            jnp.stack([qkv_part.astype(jnp.bfloat16)] * lax.axis_size("seq")), "seq", 0, 0
+        ),
+        axis=1,
+    )
     head_cols = HEADS * HD
     queries = projected[:, :head_cols].reshape(requests, steps_each, HEADS, HD)
     new_keys = projected[:, head_cols : 2 * head_cols].reshape(requests, steps_each, HEADS, HD)

time: 532 us -> 523 us (0.983)
  blocking collectives: 179 us -> 155 us
  waiting for transfers between devices: 195 us -> 205 us
  starting transfers between devices: 7.46 us -> 13.7 us
    all_gather x1 -> x0, blocking collectives: 24.2 us -> none  [body(): lax.all_gather(qkv_part.astype(jnp.bfloat16), 'seq', axis=1, tiled=True)]
    all_to_all x0 -> x1, waiting for transfers between devices: none -> 8.54 us  [body(): lax.all_to_all(jnp.stack([qkv_part.astype(jnp.bfloat16)] * lax.axis_size(...]
    all_to_all x0 -> x1, starting transfers between devices: none -> 6.05 us  [body(): lax.all_to_all(jnp.stack([qkv_part.astype(jnp.bfloat16)] * lax.axis_size(...]
  transfers between devices with their start and end apart: 7 -> 8, of which waited for: 5 -> 6; matrix products, arithmetic and copies ran while one was open for 10% -> 9% of each run, Pallas kernels for 0% -> 0%
where the time goes in v1:
time: 523 us; the launch traced here: 520 us
  waiting for transfers between devices  205 us (39%)
  blocking collectives  155 us (30%)
  local copies, waits for them, and re-layouts  66.2 us (13%)
  other arithmetic  40 us (8%)
  matrix products  26 us (5%)
  between operations  14.2 us (3%)
  starting transfers between devices  13.7 us (3%)
    psum x1, waiting for transfers between devices, body(): mixed_sum = lax.psum(projected_out, 'seq')  81.6 us
    psum x1, blocking collectives, body(): everywhere = lax.psum(looked, ('seq', 'req'))  74.1 us
    unnamed x6, waiting for transfers between devices  72.8 us
    all_gather x2, blocking collectives, merged_2(): everything = jax.tree.map(lambda part: lax.all_gather(part, axis), array)  44.8 us
    psum x1, waiting for transfers between devices, body(): lax.psum((jnp.dot(second_spread_state, gate_weight, preferred_element_typ...  34.3 us
    psum x1, blocking collectives, body(): lax.psum((jnp.dot(second_spread_state, gate_weight, preferred_element_typ...  24.2 us
    dynamic_slice x15, local copies, waits for them, and re-layouts, hop(): return combine(so_far, jax.tree.map(lambda part: part[k], everything))  14.7 us
    reshape x1, local copies, waits for them, and re-layouts, body(): cache_v = cached_value_pages.reshape(slots * page_len, HEADS, HD)  13.2 us
  transfers between devices with their start and end apart: 8, of which 6 were waited for; matrix products, arithmetic and copies ran while one was open for 9% of the time, Pallas kernels for 0%

profile of v1, /device:TPU:0, one launch (start us, length us, event | category | flops | bytes accessed | tf_op | source)
XLA Modules:
  0.0 520.1 jit_solution(4751846097289351558)
XLA Ops:
  7.4 4.9 gather_fusion
  12.2 2.8 convert_select_fusion
  15.0 74.1 %all-reduce.12 = bf16[128,3584]{1,0:T(8,128)(2,1)} all-reduce(f32[128,3584]{1,0:T(8,128)} %convert_select_fusion), channel_id=1, replica_groups=mesh['seq'=16,'req'=8] {'seq','req'}, use_global_device_ids=true, to_apply=%region_0.1 | all-reduce | flops 458752 | bytes 2752512 | tf_op jit(solution)/shard_map/psum | solution.py:91
  92.9 1.0 multiply_convert_fusion
  94.6 3.9 all-to-all-start
  100.2 1.5 fusion.55
  102.3 1.3 add_convert_fusion.2
  103.6 2.0 all-to-all-done
  105.7 2.6 fusion.67
  109.8 13.1 %reshape.195 = bf16[768,16,224]{2,1,0:T(8,128)(2,1)} reshape(bf16[6,1,128,3584]{3,2,1,0:T(8,128)(2,1)} %param.24) | data formatting | bytes 11010048 | tf_op jit(solution)/shard_map/reshape | solution.py:118
  122.9 13.2 %reshape.196 = bf16[768,16,224]{2,1,0:T(8,128)(2,1)} reshape(bf16[6,1,128,3584]{3,2,1,0:T(8,128)(2,1)} %param.25) | data formatting | bytes 11010048 | tf_op jit(solution)/shard_map/reshape | solution.py:119
  138.6 6.0 %all-to-all-start.1 = ((bf16[16,16,672]{2,1,0:T(8,128)(2,1)}), bf16[16,16,672]{2,1,0:T(8,128)(2,1)}, u32[]{:S(2)}, u32[]{:S(2)}) async-start(bf16[16,16,672]{2,1,0:T(8,128)(2,1)} %stack.2), calls=%async_computation.2 | async-start | bytes 786432 | tf_op jit(solution)/shard_map/all_to_all | solution.py:104
  145.6 8.5 %all-to-all-done.1 = bf16[16,16,672]{2,1,0:T(8,128)(2,1)} async-done(((bf16[16,16,672]{2,1,0:T(8,128)(2,1)}), bf16[16,16,672]{2,1,0:T(8,128)(2,1)}, u32[]{:S(2)}, u32[]{:S(2)}) %all-to-all-start.1) | async-done | bytes 344096 | tf_op jit(solution)/shard_map/all_to_all | solution.py:104
  154.1 1.9 copy.112
  156.0 1.5 reshape.194
  158.4 1.1 reshape.201
  160.3 1.1 reshape.200
  161.5 1.3 subtract_convert_fusion
  162.9 6.8 %select_reduce_fusion = (f32[4,4,16]{1,0,2:T(4,128)S(1)}, f32[4,4,16,768]{3,1,0,2:T(4,128)S(1)}) fusion(pred[4,768]{1,0:T(4,128)(4,1)} %fusion.54, bf16[768,16,224,1]{2,1,0,3:T(8,128)(2,1)} %bitcast.110, bf16[4,4,16,112]{3,1,0,2:T(4,128)(2,1)S(1)} %get-tuple-element.268, bf16[4,4,16,112]{3,1,0,2:T(4,128)(2,1)S(1)} %get-tuple-element.269), kind=kOutput, calls=%fused_computation.25 | convolution fusion | flops 88899328 | bytes 6410240 | tf_op jit(solution)/shard_map/rthd,khd->rthk/dot_general | solution.py:134
  170.7 4.6 fusion.16
  176.5 2.3 fusion.21
  179.6 21.5 %all-gather.1 = f32[64,4,16]{2,1,0:T(4,128)S(1)} all-gather(f32[4,4,16]{2,1,0:T(4,128)S(1)} %copy.117), channel_id=3, replica_groups=mesh['seq'=16,'req'=8] {'seq'}, dimensions={0}, use_global_device_ids=true | all-gather | bytes 17408 | tf_op jit(solution)/shard_map/all_gather | solution.py:15
  201.2 23.3 %all-gather = f32[64,4,16]{2,1,0:T(4,128)S(1)} all-gather(f32[4,4,16]{2,1,0:T(4,128)} %copy.116), channel_id=2, replica_groups=mesh['seq'=16,'req'=8] {'seq'}, dimensions={0}, use_global_device_ids=true | all-gather | bytes 17408 | tf_op jit(solution)/shard_map/all_gather | solution.py:15
  224.5 1.2 pad_maximum_fusion.1
  226.5 1.1 copy.127
  233.0 29.8 %while.19 = (s32[]{:T(128)}, f32[4,4,16]{2,1,0:T(4,128)S(1)}, f32[4,4,16]{2,1,0:T(4,128)S(1)}, f32[4,4,16,224]{3,2,1,0:T(8,128)S(1)}, f32[16,4,4,16]{3,2,1,0:T(4...) while((s32[]{:T(128)}, f32[4,4,16]{2,1,0:T(4,128)S(1)}, ...), condition=%wide.region_8.9_spmd, body=%wide.region_7.8_spmd.sunk | while | flops 173573 | bytes 1157271 | solution.py:21
  233.8 1.0 constant_dynamic-slice_fusion.5
  235.7 1.0 constant_dynamic-slice_fusion.5
  237.7 1.0 constant_dynamic-slice_fusion.5
  239.7 1.0 constant_dynamic-slice_fusion.5
  241.7 1.0 constant_dynamic-slice_fusion.5
  253.6 1.0 constant_dynamic-slice_fusion.5
  261.6 1.0 constant_dynamic-slice_fusion.5
  264.8 1.3 fusion.68
  266.2 81.6 %all-reduce.7.cloned.1.call-done = f32[16,7168]{1,0:T(8,128)} async-done(((f32[16,7168]{1,0:T(8,128)}), f32[16,7168]{1,0:T(8,128)}) %all-reduce.7.cloned.1.call-update) | async-done | bytes 458768 | tf_op jit(solution)/shard_map/psum | solution.py:174
  347.8 1.3 fusion.24
  349.3 11.4 %all_to_all.59 = bf16[16,8,896]{2,0,1:T(8,128)(2,1)S(1)} all-to-all(bf16[16,8,896]{2,0,1:T(8,128)(2,1)S(1)} %bitcast.118), channel_id=1, replica_groups=mesh['seq'=16,'req'=8] {'req'}, dimensions={1} | all-to-all | bytes 458752 | tf_op jit(solution)/shard_map/all_to_all | solution.py:179
  360.7 1.2 fusion.69
  362.0 1.2 fusion.71
  363.3 1.2 fusion.70
  364.4 24.2 %psum.38 = bf16[128,128]{1,0:T(8,128)(2,1)S(1)} all-reduce(f32[128,128]{1,0:T(8,128)S(1)} %fusion.70), channel_id=1, replica_groups=mesh['seq'=16,'req'=8] {'req'}, use_global_device_ids=true, to_apply=%region_14.15 | all-reduce | flops 16384 | bytes 98304 | tf_op jit(solution)/shard_map/psum | solution.py:181
  388.6 34.3 %all-reduce.11.cloned.1.call-done = (f32[128,896]{1,0:T(8,128)}, f32[128,896]{1,0:T(8,128)}) async-done(((f32[128,896]{1,0:T(8,128)}, f32[128,896]{1,0:T(8,128)}), (f32[128,896]{1,0:T(8,128)}, f32[128,896]{1,0:T(8,128)})) %all-reduce.11.cloned.1.call-update) | async-done | bytes 917520 | tf_op jit(solution)/shard_map/psum | solution.py:181
  422.9 2.1 convolution_add_fusion.1
  425.1 3.2 fusion.19
  429.0 3.4 all-to-all-start.2
  433.7 5.9 %all-to-all-done.2 = bf16[16,8,896]{2,0,1:T(8,128)(2,1)S(1)} async-done(((bf16[16,8,896]{2,0,1:T(8,128)(2,1)}), bf16[16,8,896]{2,0,1:T(8,128)(2,1)S(1)}, u32[]{:S(2)}, u32[]{:S(2)}) %all-to-all-start.2) | async-done | bytes 229408 | tf_op jit(solution)/shard_map/all_to_all | solution.py:178
  439.5 72.7 %all-reduce.9.cloned.1.call-done = f32[128,896]{1,0:T(8,128)} async-done(((f32[128,896]{1,0:T(8,128)}), f32[128,896]{1,0:T(8,128)}) %all-reduce.9.cloned.1.call-update) | async-done | bytes 458768
  512.2 1.4 fusion.45
  (153 shorter events, 49.7 us)
Async XLA Ops:
  6.5 258.2 %copy-start = (bf16[224,7168]{1,0:T(8,128)(2,1)S(1)}, bf16[224,7168]{1,0:T(8,128)(2,1)}, u32[]{:S(2)}) copy-start(bf16[224,7168]{1,0:T(8,128)(2,1)} %param.28) | copy-start | bytes 9633796
  15.0 75.1 %copy-start.7 = (bf16[16,3584]{1,0:T(8,128)(2,1)S(1)}, bf16[16,3584]{1,0:T(8,128)(2,1)}, u32[]{:S(2)}) copy-start(bf16[16,3584]{1,0:T(8,128)(2,1)} %param.20) | copy-start | bytes 344068
  90.0 18.2 %copy-start.3 = (bf16[16,3584]{1,0:T(8,128)(2,1)}, bf16[16,3584]{1,0:T(8,128)(2,1)S(1)}, u32[]{:S(2)}) copy-start(bf16[16,3584]{1,0:T(8,128)(2,1)S(1)} %dynamic-slice_convert_fusion) | copy-start | bytes 344068
  94.6 11.0 %all-to-all-start = ((bf16[16,8,896]{2,0,1:T(8,128)(2,1)}), bf16[16,8,896]{2,0,1:T(8,128)(2,1)S(1)}, u32[]{:S(2)}, u32[]{:S(2)}) async-start(bf16[16,8,896]{2,0,1:T(8,128)(2,1)} %copy.111), calls=%async_computation | async-start | bytes 458752 | tf_op jit(solution)/shard_map/all_to_all | solution.py:95
  98.5 38.5 %reduce-scatter.2.cloned.1.call-start = ((), (), s32[]{:S(2)}) async-start(), calls=%async_computation.5 | async-start | bytes 442368 | tf_op jit(solution)/shard_map/reduce_scatter | solution.py:97
  122.9 13.3 %copy-start.18 = (f32[4,4]{1,0:T(4,128)S(1)}, f32[4,4]{1,0:T(4,128)}, u32[]{:S(2)}) copy-start(f32[4,4]{1,0:T(4,128)} %add_convert_fusion.2) | copy-start | bytes 196
  122.9 21.9 %copy-start.19 = (s32[4]{0:T(128)S(1)}, s32[4]{0:T(128)}, u32[]{:S(2)}) copy-start(s32[4]{0:T(128)} %param.26) | copy-start | bytes 52
  138.6 15.5 %all-to-all-start.1 = ((bf16[16,16,672]{2,1,0:T(8,128)(2,1)}), bf16[16,16,672]{2,1,0:T(8,128)(2,1)}, u32[]{:S(2)}, u32[]{:S(2)}) async-start(bf16[16,16,672]{2,1,0:T(8,128)(2,1)} %stack.2), calls=%async_computation.2 | async-start | bytes 786432 | tf_op jit(solution)/shard_map/all_to_all | solution.py:104
  144.6 87.2 %all-gather.5.cloned.1.call-start = ((), (), s32[]{:S(2)}) async-start(), calls=%async_computation.7 | async-start | bytes 4456448 | tf_op jit(solution)/shard_map/all_gather | solution.py:15
  158.4 3.1 copy-start.14
  158.4 3.1 copy-start.15
  161.5 9.2 %slice-start = ((s8[6291456]{0:T(1024)(128)(4,1)}), s8[4194304]{0:T(1024)(128)(4,1)S(1)}, s32[]{:S(2)}) async-start(s8[6291456]{0:T(1024)(128)(4,1)} %bitcast.107), calls=%async_computation.10 | async-start | bytes 8388608
  162.8 6.9 %copy-start.11 = (bf16[4,4,16,112]{3,1,0,2:T(4,128)(2,1)}, bf16[4,4,16,112]{3,1,0,2:T(4,128)(2,1)S(1)}, u32[]{:S(2)}) copy-start(bf16[4,4,16,112]{3,1,0,2:T(4,128)(2,1)S(1)} %get-tuple-element.269) | copy-start | bytes 172036
  162.9 7.8 %slice-start.1 = ((s8[6291456]{0:T(1024)(128)(4,1)}), s8[2097152]{0:T(1024)(128)(4,1)S(1)}, s32[]{:S(2)}) async-start(s8[6291456]{0:T(1024)(128)(4,1)} %bitcast.107), calls=%async_computation.11 | async-start | bytes 4194304
  162.9 7.8 %copy-start.17 = (pred[4,768]{1,0:T(4,128)(4,1)S(1)}, pred[4,768]{1,0:T(4,128)(4,1)}, u32[]{:S(2)}) copy-start(pred[4,768]{1,0:T(4,128)(4,1)} %fusion.54) | copy-start | bytes 9220
  169.7 0.9 copy-start.9
  175.2 55.5 %copy-start.10 = (bf16[16,3584]{1,0:T(8,128)(2,1)S(1)}, bf16[16,3584]{1,0:T(8,128)(2,1)}, u32[]{:S(2)}) copy-start(bf16[16,3584]{1,0:T(8,128)(2,1)} %get-tuple-element.255) | copy-start | bytes 344068
  175.3 172.5 %all-reduce.7.cloned.1.call-start = ((), (), s32[]{:S(2)}) async-start(), calls=%async_computation.6 | async-start | bytes 917504 | tf_op jit(solution)/shard_map/psum | solution.py:174
  201.1 24.5 %copy-start.12 = (f32[64,4,16]{2,1,0:T(4,128)}, f32[64,4,16]{2,1,0:T(4,128)S(1)}, u32[]{:S(2)}) copy-start(f32[64,4,16]{2,1,0:T(4,128)S(1)} %all-gather.1) | copy-start | bytes 49156
  224.5 1.2 copy-start.13
  264.8 1.4 copy-start.16
  264.8 83.0 %copy-start.4 = (bf16[16,3584]{1,0:T(8,128)(2,1)S(1)}, bf16[16,3584]{1,0:T(8,128)(2,1)}, u32[]{:S(2)}) copy-start(bf16[16,3584]{1,0:T(8,128)(2,1)} %copy-done.3) | copy-start | bytes 344068
  264.8 83.0 %copy-start.8 = (bf16[16,3584]{1,0:T(8,128)(2,1)S(1)}, bf16[16,3584]{1,0:T(8,128)(2,1)}, u32[]{:S(2)}) copy-start(bf16[16,3584]{1,0:T(8,128)(2,1)} %param.20) | copy-start | bytes 344068
  266.1 156.8 %all-reduce.11.cloned.1.call-start = ((), (), s32[]{:S(2)}) async-start(), calls=%async_computation.9 | async-start | bytes 1835008 | tf_op jit(solution)/shard_map/psum | solution.py:181
  347.8 12.9 %copy-start.5 = (bf16[896,896]{1,0:T(8,128)(2,1)S(1)}, bf16[896,896]{1,0:T(8,128)(2,1)}, u32[]{:S(2)}) copy-start(bf16[896,896]{1,0:T(8,128)(2,1)} %param.30) | copy-start | bytes 4816900
  349.1 12.8 %copy-start.1 = (bf16[16,7168]{1,0:T(8,128)(2,1)}, bf16[16,7168]{1,0:T(8,128)(2,1)S(1)}, u32[]{:S(2)}) copy-start(bf16[16,7168]{1,0:T(8,128)(2,1)S(1)} %get-tuple-element.249) | copy-start | bytes 688132
  349.1 12.8 %copy-start.6 = (bf16[896,896]{1,0:T(8,128)(2,1)S(1)}, bf16[896,896]{1,0:T(8,128)(2,1)}, u32[]{:S(2)}) copy-start(bf16[896,896]{1,0:T(8,128)(2,1)} %param.31) | copy-start | bytes 4816900
  363.2 149.0 %all-reduce.9.cloned.1.call-start = ((), (), s32[]{:S(2)}) async-start(), calls=%async_computation.8 | async-start | bytes 917504
  425.1 3.2 copy-start.2
  425.1 7.3 %copy-start.20 = (u32[128]{0:T(128)S(1)}, u32[128]{0:T(128)}, u32[]{:S(2)}) copy-start(u32[128]{0:T(128)} %constant.127) | copy-start | bytes 1540
  429.0 10.5 %all-to-all-start.2 = ((bf16[16,8,896]{2,0,1:T(8,128)(2,1)}), bf16[16,8,896]{2,0,1:T(8,128)(2,1)S(1)}, u32[]{:S(2)}, u32[]{:S(2)}) async-start(bf16[16,8,896]{2,0,1:T(8,128)(2,1)} %bitcast.116), calls=%async_computation.3 | async-start | bytes 458752 | tf_op jit(solution)/shard_map/all_to_all | solution.py:178
Sparse Core Ops, SparseCore 0:
  108.4 27.5 reduce-scatter.1
  175.4 48.4 all-gather.4
  266.3 81.4 all-reduce.6
  363.4 59.5 all-reduce.10
  428.4 83.7 all-reduce.8
